TPU v7x, 256 devices: a whole 4x4x8 slice. The times are simulated.
256 devices in a mesh: wide: 32 (over z, y), narrow: 8 (over x, core).
Axes of the slice: x: 4, y: 4, z: 8, core: 2. Of those that a mesh axis runs over, the one named last changes fastest.
Arguments:
- hidden: bfloat16 [160, 4096], P('wide', 'narrow'), may hold values from -18 to 18
- w_query: bfloat16 [4096, 4096], P('narrow', 'wide'), may hold values from -0.09375 to 0.09375
- w_keyval: bfloat16 [4096, 1024], P('narrow', 'wide'), may hold values from -0.09375 to 0.09375
- w_out: bfloat16 [4096, 4096], P('narrow', 'wide'), may hold values from -0.09375 to 0.09375
- pool: bfloat16 [16384, 16, 1024], P(('wide', 'narrow')), may hold values from -144 to 144
- page_req: int32 [16384], P(('wide', 'narrow')), may hold values from -1 to 31, as said below
- page_idx: int32 [16384], P(('wide', 'narrow')), may hold values from -1 to 511, as said below
- lengths: int32 [32], replicated, may hold values from 128 to 8192, as said below
- moves: int32 [16384, 1], P(('wide', 'narrow')), may hold values from 0 to 31; in each aligned block of 64 rows (0 to 63, 64 to 127, ...) at most 2 rows name the same one
- accepted: int32 [32], replicated, may hold values from 1 to 5
Outputs:
- attended: bfloat16 [160, 4096], P('narrow', 'wide')
- new_entries: bfloat16 [32, 5, 1024], P('wide')
- moved_pool: bfloat16 [16384, 16, 1024], P(('wide', 'narrow'))
- moved_req: int32 [16384], P(('wide', 'narrow'))
- moved_idx: int32 [16384], P(('wide', 'narrow'))
Inputs may be any that keep to these rules, and one draw needn't show every extreme that they name: Request r holds exactly ceil(lengths[r] / 16) slots, whose page numbers are 0 up to that count minus 1, each once; every other slot is free, with page_req and page_idx -1. `page_idx`: see page_req. `lengths`: each length lies either in 128 to 256 or in 6144 to 8192; exactly 16 lie in the second range. `moves`: each device sends exactly 2 of its slots to each index of wide.
All inputs are finite; a program needn't handle non-finite values.
Results may differ from a plain program's by a relative error of at most 0.03.
Values may be sent and summed in bfloat16 or wider, within the bound.
A program may use at most 128 MiB of HBM per device.

v0:
```python
import math
import jax
import jax.numpy as jnp
from jax import lax
from jax.sharding import PartitionSpec as P

HEADS = 32
KVH = 4
HD = 128
STEPS = 5
PAGE = 16
NEG_FILL = -1e30


def combine(first, second):
    peak = jnp.maximum(first[0], second[0])
    lead = jnp.exp(first[0] - peak)
    trail = jnp.exp(second[0] - peak)
    return (
        peak,
        first[1] * lead + second[1] * trail,
        first[2] * lead[..., None] + second[2] * trail[..., None],
    )


def on_device(hidden, w_query, w_keyval, w_out, pool, page_req, page_idx, lengths, moves, accepted):
    wide_count = lax.axis_size("wide")
    narrow_count = lax.axis_size("narrow")
    groups = HEADS // KVH
    scale = 1.0 / math.sqrt(HD)
    rows_all = lax.all_gather(hidden, "wide", axis=0, tiled=True)
    total_rows = rows_all.shape[0]
    req_total = total_rows // STEPS
    joined = jnp.concatenate([w_query, w_keyval], axis=1)
    query_cols = w_query.shape[1]
    picked = rows_all
    projected = lax.psum_scatter(
        jnp.dot(picked, joined, preferred_element_type=jnp.float32),
        "narrow",
        scatter_dimension=0,
        tiled=True,
    ).astype(jnp.bfloat16)
    query_rows, keyval_rows = (
        lax.all_gather(projected[:, :query_cols], "narrow", axis=0, tiled=True),
        lax.all_gather(projected[:, query_cols:], "narrow", axis=0, tiled=True),
    )
    query_full, keyval_full = (
        lax.all_gather(query_rows, "wide", axis=1, tiled=True),
        lax.all_gather(keyval_rows, "wide", axis=1, tiled=True),
    )
    query = query_full.reshape(req_total, STEPS, KVH, groups, HD)
    keyval = keyval_full.reshape(req_total, STEPS, 2, KVH, HD)
    pool_size = pool.shape[0]
    capacity = pool_size // wide_count
    dest = moves[:, 0]
    order = jnp.arange(pool_size, dtype=jnp.int32)
    rank = jnp.sum((dest[:, None] == dest[None, :]) & (order[None, :] < order[:, None]), axis=1)
    target = dest * capacity + rank
    source_of = jnp.sum(jnp.where(target[None, :] == order[:, None], order[None, :], 0), axis=1)
    moved = (
        lax.all_to_all(
            jnp.take(pool, source_of, axis=0), "wide", split_axis=0, concat_axis=0, tiled=True
        ),
        lax.all_to_all(
            jnp.take(page_req, source_of), "wide", split_axis=0, concat_axis=0, tiled=True
        ),
        lax.all_to_all(
            jnp.take(page_idx, source_of), "wide", split_axis=0, concat_axis=0, tiled=True
        ),
    )
    pages = moved[0]
    requests = moved[1]
    count = pages.shape[0]
    owners = jnp.maximum(requests, 0)
    cache = pages.reshape(count, PAGE, 2, KVH, HD)
    page_query = jnp.take(query, owners, axis=0)
    scores = (
        jnp.einsum(
            "pskgd,ptkd->pkgst", page_query, cache[:, :, 0], preferred_element_type=jnp.float32
        )
        * scale
    )
    positions = moved[2][:, None] * PAGE + jnp.arange(PAGE, dtype=jnp.int32)[None, :]
    visible = (positions < jnp.take(lengths, owners)[:, None]) & (requests >= 0)[:, None]
    visible = visible[:, None, None, None, :]
    scores = jnp.where(visible, scores, NEG_FILL)
    peaks = jnp.max(scores, axis=-1)
    weights = jnp.where(visible, jnp.exp(scores - peaks[..., None]), 0.0)
    totals = jnp.sum(weights, axis=-1)
    sums = jnp.einsum(
        "pkgst,ptkd->pkgsd",
        weights.astype(jnp.bfloat16),
        cache[:, :, 1],
        preferred_element_type=jnp.float32,
    )
    member = requests[None, :] == jnp.arange(req_total, dtype=jnp.int32)[:, None]
    req_peaks = jnp.max(jnp.where(member[:, :, None, None, None], peaks[None], NEG_FILL), axis=1)
    factor = jnp.exp(peaks - jnp.take(req_peaks, owners, axis=0))
    selector = member.astype(jnp.float32)
    req_totals = jnp.dot(
        selector, (totals * factor).reshape(count, -1), precision=lax.Precision.HIGHEST
    )
    req_sums = jnp.dot(
        selector, (sums * factor[..., None]).reshape(count, -1), precision=lax.Precision.HIGHEST
    )
    req_totals = req_totals.reshape(req_total, KVH, groups, STEPS)
    req_sums = req_sums.reshape(req_total, KVH, groups, STEPS, HD)
    row_peaks = jnp.transpose(req_peaks, (0, 3, 1, 2)).reshape(total_rows, HEADS)
    row_totals = jnp.transpose(req_totals, (0, 3, 1, 2)).reshape(total_rows, HEADS)
    row_sums = jnp.transpose(req_sums, (0, 3, 1, 2, 4)).reshape(total_rows, HEADS, HD)
    state = (row_peaks, row_totals, row_sums)
    fresh_scores = (
        jnp.einsum("rskgd,rtkd->rkgst", query, keyval[:, :, 0], preferred_element_type=jnp.float32)
        * scale
    )
    causal = jnp.arange(STEPS)[None, :] <= jnp.arange(STEPS)[:, None]
    fresh_scores = jnp.where(causal, fresh_scores, NEG_FILL)
    fresh_peaks = jnp.max(fresh_scores, axis=-1)
    fresh_weights = jnp.where(causal, jnp.exp(fresh_scores - fresh_peaks[..., None]), 0.0)
    fresh_totals = jnp.sum(fresh_weights, axis=-1)
    fresh_sums = jnp.einsum(
        "rkgst,rtkd->rskgd",
        fresh_weights.astype(jnp.bfloat16),
        keyval[:, :, 1],
        preferred_element_type=jnp.float32,
    )
    self_peaks = jnp.transpose(fresh_peaks, (0, 3, 1, 2)).reshape(total_rows, HEADS)
    self_totals = jnp.transpose(fresh_totals, (0, 3, 1, 2)).reshape(total_rows, HEADS)
    self_sums = fresh_sums.reshape(total_rows, HEADS, HD)
    head_count = HEADS // narrow_count
    first_head = lax.axis_index("narrow") * head_count
    mine_peaks = lax.dynamic_slice_in_dim(self_peaks, first_head, head_count, 1)
    mine_totals = lax.dynamic_slice_in_dim(self_totals, first_head, head_count, 1)
    mine_sums = lax.dynamic_slice_in_dim(self_sums, first_head, head_count, 1)
    peak_all = lax.pmax(state[0], ("wide", "narrow"))
    lead = jnp.exp(state[0] - peak_all)
    scaled_sums = (state[2] * lead[..., None]).reshape(total_rows, HEADS * HD)
    part_sums, part_totals = (
        lax.psum_scatter(
            scaled_sums.astype(jnp.bfloat16), "narrow", scatter_dimension=1, tiled=True
        ).astype(jnp.float32),
        lax.psum_scatter(
            (state[1] * lead).astype(jnp.bfloat16), "narrow", scatter_dimension=1, tiled=True
        ).astype(jnp.float32),
    )
    full_sums, full_totals = (
        lax.psum(part_sums.astype(jnp.bfloat16), "wide").astype(jnp.float32),
        lax.psum(part_totals.astype(jnp.bfloat16), "wide").astype(jnp.float32),
    )
    block_peaks = lax.dynamic_slice_in_dim(peak_all, first_head, head_count, 1)
    final = combine(
        (block_peaks, full_totals, full_sums.reshape(total_rows, head_count, HD)),
        (mine_peaks, mine_totals, mine_sums),
    )
    attn_block = (
        (final[2] / final[1][..., None]).reshape(total_rows, head_count * HD).astype(jnp.bfloat16)
    )
    picked = attn_block
    attended = lax.psum_scatter(
        jnp.dot(picked, w_out, preferred_element_type=jnp.float32).astype(jnp.bfloat16),
        "narrow",
        scatter_dimension=0,
        tiled=True,
    )
    local_req = hidden.shape[0] // STEPS
    first_req = lax.axis_index("wide") * local_req
    fresh_rows = lax.dynamic_slice_in_dim(
        keyval_full.reshape(req_total, STEPS, -1), first_req, local_req, 0
    )
    kept = lax.dynamic_slice_in_dim(accepted, first_req, local_req, 0)
    step_ids = jnp.arange(STEPS, dtype=jnp.int32)
    new_entries = jnp.where(
        step_ids[None, :, None] < kept[:, None, None], fresh_rows, jnp.zeros((), jnp.bfloat16)
    )
    return (attended, new_entries, moved[0], moved[1], moved[2])


def solution(mesh):
    in_specs = (
        P("wide", "narrow"),
        P("narrow", "wide"),
        P("narrow", "wide"),
        P("narrow", "wide"),
        P(("wide", "narrow"), None, None),
        P(("wide", "narrow")),
        P(("wide", "narrow")),
        P(),
        P(("wide", "narrow"), None),
        P(),
    )
    out_specs = (
        P("narrow", "wide"),
        P("wide", None, None),
        P(("wide", "narrow"), None, None),
        P(("wide", "narrow")),
        P(("wide", "narrow")),
    )
    return jax.shard_map(
        on_device, mesh=mesh, in_specs=in_specs, out_specs=out_specs, check_vma=False
    )
```

profile of v0, /device:TPU:8, one launch (start us, length us, event | category | flops | bytes accessed | tf_op | source)
XLA Modules:
  0.0 752.8 jit_solution(15309788727797275602)
XLA Ops:
  12.6 11.7 %all-to-all-start = ((s32[32,2,1]{1,2,0:T(1,128)}), s32[32,2,1]{1,2,0:T(1,128)S(1)}, u32[]{:S(2)}, u32[]{:S(2)}) async-start(s32[32,2,1]{1,2,0:T(1,128)} %bitcast.1), calls=%async_computation | async-start | bytes 32768 | tf_op jit(solution)/shard_map/all_to_all | solution.py:64
  27.0 5.7 all-to-all-done
  32.7 5.0 all-to-all-start.1
  40.9 5.4 all-to-all-done.1
  46.3 5.6 all-to-all-start.2
  52.0 86.4 %all-gather = bf16[32,5,512]{2,1,0:T(8,128)(2,1)S(1)} all-gather(bf16[1,5,512]{2,1,0:T(8,128)(2,1)S(1)} %bitcast.133), channel_id=1, replica_groups=mesh['wide'=32,'narrow'=8] {'wide'}, dimensions={0}, use_global_device_ids=true | all-gather | bytes 168960 | tf_op jit(solution)/shard_map/all_gather | solution.py:31
  140.1 25.1 %all-reduce = bf16[160,160]{0,1:T(8,128)(2,1)S(1)} all-reduce(f32[160,160]{0,1:T(8,128)S(1)} %convolution_bitcast_fusion.1), channel_id=2, replica_groups=mesh['wide'=32,'narrow'=8] {'narrow'}, use_global_device_ids=true, to_apply=%region_2.0.clone | all-reduce | flops 25600 | bytes 153600
  165.4 12.8 %all-gather.1 = bf16[8,20,128]{2,1,0:T(8,128)(2,1)S(1)} all-gather(bf16[1,20,128]{2,1,0:T(8,128)(2,1)S(1)} %copy.106), channel_id=1, replica_groups=mesh['wide'=32,'narrow'=8] {'narrow'}, dimensions={0}, use_global_device_ids=true | all-gather | bytes 46080 | tf_op jit(solution)/shard_map/all_gather | solution.py:44
  182.6 66.8 %all-gather.5.cloned.1.call-done = bf16[160,4096]{1,0:T(8,128)(2,1)} async-done(((bf16[160,128]{1,0:T(8,128)(2,1)}), bf16[160,4096]{1,0:T(8,128)(2,1)}) %all-gather.5.cloned.1.call-update) | async-done | bytes 1310736 | tf_op jit(solution)/shard_map/all_gather | solution.py:48
  253.4 4.4 reshape.221
  270.6 6.2 fusion.4
  279.7 75.1 %pmax.7 = f32[160,32]{0,1:T(8,128)S(1)} all-reduce(f32[160,32]{0,1:T(8,128)S(1)} %copy.119), channel_id=1, replica_groups=mesh['wide'=32,'narrow'=8] {'wide','narrow'}, use_global_device_ids=true, to_apply=%region_5.7 | all-reduce | flops 5120 | bytes 40960 | tf_op jit(solution)/shard_map/pmax | solution.py:135
  357.6 5.5 broadcast_multiply_fusion
  363.1 5.1 copy.114
  368.2 6.7 reshape.223
  374.9 7.3 dot_general.39
  382.3 8.2 %fusion.17 = f32[32,5,4,8,128]{4,0,1,3,2:T(8,128)S(1)} fusion(f32[4,8,5,128,64]{3,2,1,0,4:T(8,128)} %dot_general.39, s32[64]{0:T(128)S(1)} %eq.48), kind=kOutput, calls=%fused_computation.30 | convolution fusion | flops 503318528 | bytes 7864576 | tf_op jit(solution)/shard_map/dot_general | solution.py:103
  402.7 12.8 %all-gather.2 = bf16[8,20,32]{2,1,0:T(8,128)(2,1)S(1)} all-gather(bf16[1,20,32]{2,1,0:T(8,128)(2,1)S(1)} %copy.121), channel_id=1, replica_groups=mesh['wide'=32,'narrow'=8] {'narrow'}, dimensions={0}, use_global_device_ids=true | all-gather | bytes 11520 | tf_op jit(solution)/shard_map/all_gather | solution.py:45
  415.6 47.0 %all_gather.19 = bf16[160,1024]{0,1:T(8,128)(2,1)S(1)} all-gather(bf16[160,32]{0,1:T(8,128)(2,1)S(1)} %copy.155), channel_id=1, replica_groups=mesh['wide'=32,'narrow'=8] {'wide'}, dimensions={1}, use_global_device_ids=true | all-gather | bytes 337920 | tf_op jit(solution)/shard_map/all_gather | solution.py:49
  465.8 6.4 fusion.20
  481.1 23.9 %all-reduce.1 = bf16[160,32]{1,0:T(8,128)(2,1)S(1)} all-reduce(bf16[160,32]{1,0:T(8,128)(2,1)S(1)} %copy.142), channel_id=4, replica_groups=mesh['wide'=32,'narrow'=8] {'narrow'}, use_global_device_ids=true, to_apply=%region_10.12.clone | all-reduce | flops 5120 | bytes 20480
  505.2 72.1 %psum.15 = bf16[160,4]{0,1:T(4,128)(2,1)S(1)} all-reduce(bf16[160,4]{0,1:T(4,128)(2,1)S(1)} %copy.143), channel_id=1, replica_groups=mesh['wide'=32,'narrow'=8] {'wide'}, use_global_device_ids=true, to_apply=%region_11.13 | all-reduce | flops 640 | bytes 2560 | tf_op jit(solution)/shard_map/psum | solution.py:148
  579.4 136.8 %all-reduce.5.cloned.1.call-done = bf16[160,4,128]{2,1,0:T(4,128)(2,1)} async-done(((bf16[160,4,128]{2,1,0:T(4,128)(2,1)}), bf16[160,4,128]{2,1,0:T(4,128)(2,1)}) %all-reduce.5.cloned.1.call-update) | async-done | bytes 163856 | tf_op jit(solution)/shard_map/psum | solution.py:147
  718.2 23.9 %all-reduce.2 = bf16[160,128]{1,0:T(8,128)(2,1)S(1)} all-reduce(bf16[160,128]{1,0:T(8,128)(2,1)S(1)} %convolution_convert_fusion), channel_id=5, replica_groups=mesh['wide'=32,'narrow'=8] {'narrow'}, use_global_device_ids=true, to_apply=%region_13.15.clone | all-reduce | flops 20480 | bytes 81920
  (150 shorter events, 70.9 us)
Async XLA Ops:
  7.2 17.9 %copy-start = (bf16[64,16,1024]{2,1,0:T(8,128)(2,1)S(1)}, bf16[64,16,1024]{2,1,0:T(8,128)(2,1)}, u32[]{:S(2)}) copy-start(bf16[64,16,1024]{2,1,0:T(8,128)(2,1)} %param.16) | copy-start | bytes 6291460
  12.6 20.2 %all-to-all-start = ((s32[32,2,1]{1,2,0:T(1,128)}), s32[32,2,1]{1,2,0:T(1,128)S(1)}, u32[]{:S(2)}, u32[]{:S(2)}) async-start(s32[32,2,1]{1,2,0:T(1,128)} %bitcast.1), calls=%async_computation | async-start | bytes 32768 | tf_op jit(solution)/shard_map/all_to_all | solution.py:64
  32.7 13.6 %all-to-all-start.1 = ((s32[32,2,1]{1,2,0:T(1,128)}), s32[32,2,1]{1,2,0:T(1,128)S(1)}, u32[]{:S(2)}, u32[]{:S(2)}) async-start(s32[32,2,1]{1,2,0:T(1,128)} %bitcast.4), calls=%async_computation.1 | async-start | bytes 32768 | tf_op jit(solution)/shard_map/all_to_all | solution.py:67
  40.9 11.2 %copy-start.12 = (bf16[5,512]{1,0:T(8,128)(2,1)S(1)}, bf16[5,512]{1,0:T(8,128)(2,1)}, u32[]{:S(2)}) copy-start(bf16[5,512]{1,0:T(8,128)(2,1)} %param.12) | copy-start | bytes 15364
  40.9 97.6 %copy-start.10 = (bf16[512,32]{0,1:T(8,128)(2,1)S(1)}, bf16[512,32]{0,1:T(8,128)(2,1)}, u32[]{:S(2)}) copy-start(bf16[512,32]{0,1:T(8,128)(2,1)} %param.14) | copy-start | bytes 98308
  40.9 97.8 %copy-start.18 = (u32[256]{0:T(256)S(1)}, u32[256]{0:T(256)}, u32[]{:S(2)}) copy-start(u32[256]{0:T(256)} %constant.105) | copy-start | bytes 3076
  40.9 99.0 %copy-start.16 = (bf16[512,128]{1,0:T(8,128)(2,1)S(1)}, bf16[512,128]{1,0:T(8,128)(2,1)}, u32[]{:S(2)}) copy-start(bf16[512,128]{1,0:T(8,128)(2,1)} %param.13) | copy-start | bytes 393220
  40.9 140.8 %copy-start.2 = (s32[32]{0:T(128)S(1)}, s32[32]{0:T(128)}, u32[]{:S(2)}) copy-start(s32[32]{0:T(128)} %param.19) | copy-start | bytes 388
  46.3 207.1 %all-to-all-start.2 = ((bf16[64,16,1024]{2,1,0:T(8,128)(2,1)}), bf16[64,16,1024]{2,1,0:T(8,128)(2,1)}, u32[]{:S(2)}, u32[]{:S(2)}) async-start(bf16[64,16,1024]{2,1,0:T(8,128)(2,1)} %broadcast_select_fusion.1), calls=%async_computation.2 | async-start | bytes 4194304 | tf_op jit(solution)/shard_map/all_to_all | solution.py:61
  52.0 197.5 %all-gather.5.cloned.1.call-start = ((), (), s32[]{:S(2)}) async-start(), calls=%async_computation.4 | async-start | bytes 1351680 | tf_op jit(solution)/shard_map/all_gather | solution.py:48
  165.3 84.1 %copy-start.8 = (bf16[20,160]{0,1:T(8,128)(2,1)}, bf16[20,160]{0,1:T(8,128)(2,1)S(1)}, u32[]{:S(2)}) copy-start(bf16[20,160]{0,1:T(8,128)(2,1)S(1)} %dynamic-slice_convert_fusion) | copy-start | bytes 19204
  178.9 398.4 %reduce-scatter.4.cloned.1.call-start = ((), (), s32[]{:S(2)}) async-start(), calls=%async_computation.5 | async-start | bytes 1474560 | tf_op jit(solution)/shard_map/reduce_scatter | solution.py:139
  180.8 201.5 %copy-start.11 = (s32[64]{0:T(128)}, s32[64]{0:T(128)S(1)}, u32[]{:S(2)}) copy-start(s32[64]{0:T(128)S(1)} %eq.48) | copy-start | bytes 772
  181.7 71.8 %copy-start.15 = (s32[64]{0:T(128)}, s32[64]{0:T(128)S(1)}, u32[]{:S(2)}) copy-start(s32[64]{0:T(128)S(1)} %all_to_all.21) | copy-start | bytes 772
  182.5 96.2 %copy-start.13 = (pred[64]{0:T(512)(128)(4,1)}, pred[64]{0:T(512)(128)(4,1)S(1)}, u32[]{:S(2)}) copy-start(pred[64]{0:T(512)(128)(4,1)S(1)} %get-tuple-element.22) | copy-start | bytes 196
  257.9 3.7 copy-start.6
  270.6 8.0 %copy-start.7 = (f32[64,4,8,5]{0,3,2,1:T(8,128)S(1)}, f32[64,4,8,5]{0,3,2,1:T(8,128)}, u32[]{:S(2)}) copy-start(f32[64,4,8,5]{0,3,2,1:T(8,128)} %copy.137) | copy-start | bytes 122884
  276.8 2.6 copy-start.5
  278.7 76.2 %copy-start.14 = (pred[64]{0:T(512)(128)(4,1)S(1)}, pred[64]{0:T(512)(128)(4,1)}, u32[]{:S(2)}) copy-start(pred[64]{0:T(512)(128)(4,1)} %copy-done.13) | copy-start | bytes 196
  397.5 1.7 copy-start.3
  401.8 62.0 %copy-start.17 = (s32[32]{0:T(128)S(1)}, s32[32]{0:T(128)}, u32[]{:S(2)}) copy-start(s32[32]{0:T(128)} %param.21) | copy-start | bytes 388
  401.8 314.4 %all-reduce.5.cloned.1.call-start = ((), (), s32[]{:S(2)}) async-start(), calls=%async_computation.6 | async-start | bytes 327680 | tf_op jit(solution)/shard_map/psum | solution.py:147
  479.1 238.9 %copy-start.9 = (bf16[512,128]{1,0:T(8,128)(2,1)S(1)}, bf16[512,128]{1,0:T(8,128)(2,1)}, u32[]{:S(2)}) copy-start(bf16[512,128]{1,0:T(8,128)(2,1)} %param.15) | copy-start | bytes 393220
  716.2 29.8 %copy-start.1 = (bf16[64,16,1024]{2,1,0:T(8,128)(2,1)S(1)}, bf16[64,16,1024]{2,1,0:T(8,128)(2,1)}, u32[]{:S(2)}) copy-start(bf16[64,16,1024]{2,1,0:T(8,128)(2,1)} %param.16) | copy-start | bytes 6291460
  (1 other events, 0.8 us)
Sparse Core Ops, SparseCore 0:
  179.0 70.3 all-gather.4
  401.9 30.6 reduce-scatter.3
  579.1 137.0 all-reduce.4
where the time goes:
time: 758 us; the launch traced here: 753 us
  blocking collectives  379 us (50%)
  waiting for transfers between devices  215 us (28%)
  local copies, waits for them, and re-layouts  74.7 us (10%)
  matrix products  24.9 us (3%)
  starting transfers between devices  22.9 us (3%)
  other arithmetic  20.5 us (3%)
  between operations  15.9 us (2%)
    psum x1, waiting for transfers between devices, on_device(): lax.psum(part_sums.astype(jnp.bfloat16), 'wide').astype(jnp.float32)  137 us
    all_gather x1, blocking collectives, on_device(): rows_all = lax.all_gather(hidden, 'wide', axis=0, tiled=True)  86.4 us
    pmax x1, blocking collectives, on_device(): peak_all = lax.pmax(state[0], ('wide', 'narrow'))  75.1 us
    unnamed x3, blocking collectives  73 us
    psum x1, blocking collectives, on_device(): lax.psum(part_totals.astype(jnp.bfloat16), 'wide').astype(jnp.float32)  72.1 us
    all_gather x1, waiting for transfers between devices, on_device(): lax.all_gather(query_rows, 'wide', axis=1, tiled=True)  66.8 us
    all_gather x1, blocking collectives, on_device(): lax.all_gather(keyval_rows, 'wide', axis=1, tiled=True)  47 us
  transfers between devices with their start and end apart: 6, of which 4 were waited for; matrix products, arithmetic and copies ran while one was open for 4% of the time, Pallas kernels for 0%

commit v1 on v0

--- a/solution.py
+++ b/solution.py
@@ -145,7 +145,9 @@
     )
     full_sums, full_totals = (
         lax.psum(part_sums.astype(jnp.bfloat16), "wide").astype(jnp.float32),
-        lax.psum(part_totals.astype(jnp.bfloat16), "wide").astype(jnp.float32),
+        jnp.sum(lax.all_gather(part_totals.astype(jnp.bfloat16), "wide"), axis=0).astype(
+            jnp.float32
+        ),
     )
     block_peaks = lax.dynamic_slice_in_dim(peak_all, first_head, head_count, 1)
     final = combine(

time: 758 us -> 734 us (0.968)
  blocking collectives: 379 us -> 355 us
    psum x1 -> x0, blocking collectives: 72.1 us -> none  [on_device(): lax.psum(part_totals.astype(jnp.bfloat16), 'wide').astype(jnp.float32)]
    all_gather x0 -> x1, blocking collectives: none -> 48.1 us  [on_device(): lax.all_gather(part_totals.astype(jnp.bfloat16), 'wide')]
  transfers between devices with their start and end apart: 6 -> 6, of which waited for: 4 -> 4; matrix products, arithmetic and copies ran while one was open for 4% -> 5% of each run, Pallas kernels for 0% -> 0%
where the time goes in v1:
time: 734 us; the launch traced here: 729 us
  blocking collectives  355 us (48%)
  waiting for transfers between devices  215 us (29%)
  local copies, waits for them, and re-layouts  74.7 us (10%)
  matrix products  24.9 us (3%)
  starting transfers between devices  22.9 us (3%)
  other arithmetic  20.5 us (3%)
  between operations  15.9 us (2%)
    psum x1, waiting for transfers between devices, on_device(): lax.psum(part_sums.astype(jnp.bfloat16), 'wide').astype(jnp.float32)  137 us
    all_gather x1, blocking collectives, on_device(): rows_all = lax.all_gather(hidden, 'wide', axis=0, tiled=True)  86.4 us
    pmax x1, blocking collectives, on_device(): peak_all = lax.pmax(state[0], ('wide', 'narrow'))  75.1 us
    unnamed x3, blocking collectives  73 us
    all_gather x1, waiting for transfers between devices, on_device(): lax.all_gather(query_rows, 'wide', axis=1, tiled=True)  66.8 us
    all_gather x1, blocking collectives, on_device(): lax.all_gather(part_totals.astype(jnp.bfloat16), 'wide')  48.1 us
    all_gather x1, blocking collectives, on_device(): lax.all_gather(keyval_rows, 'wide', axis=1, tiled=True)  47 us
  transfers between devices with their start and end apart: 6, of which 4 were waited for; matrix products, arithmetic and copies ran while one was open for 5% of the time, Pallas kernels for 0%

profile of v1, /device:TPU:8, one launch (start us, length us, event | category | flops | bytes accessed | tf_op | source)
XLA Modules:
  0.0 728.6 jit_solution(4761783721595958750)
XLA Ops:
  12.6 11.7 %all-to-all-start = ((s32[32,2,1]{1,2,0:T(1,128)}), s32[32,2,1]{1,2,0:T(1,128)S(1)}, u32[]{:S(2)}, u32[]{:S(2)}) async-start(s32[32,2,1]{1,2,0:T(1,128)} %bitcast.1), calls=%async_computation | async-start | bytes 32768 | tf_op jit(solution)/shard_map/all_to_all | solution.py:64
  27.0 5.7 all-to-all-done
  32.7 5.0 all-to-all-start.1
  40.9 5.4 all-to-all-done.1
  46.3 5.6 all-to-all-start.2
  52.0 86.4 %all-gather.1 = bf16[32,5,512]{2,1,0:T(8,128)(2,1)S(1)} all-gather(bf16[1,5,512]{2,1,0:T(8,128)(2,1)S(1)} %bitcast.135), channel_id=1, replica_groups=mesh['wide'=32,'narrow'=8] {'wide'}, dimensions={0}, use_global_device_ids=true | all-gather | bytes 168960 | tf_op jit(solution)/shard_map/all_gather | solution.py:31
  140.1 25.1 %all-reduce = bf16[160,160]{0,1:T(8,128)(2,1)S(1)} all-reduce(f32[160,160]{0,1:T(8,128)S(1)} %convolution_bitcast_fusion.1), channel_id=3, replica_groups=mesh['wide'=32,'narrow'=8] {'narrow'}, use_global_device_ids=true, to_apply=%region_2.0.clone | all-reduce | flops 25600 | bytes 153600
  165.4 12.8 %all-gather.2 = bf16[8,20,128]{2,1,0:T(8,128)(2,1)S(1)} all-gather(bf16[1,20,128]{2,1,0:T(8,128)(2,1)S(1)} %copy.158), channel_id=1, replica_groups=mesh['wide'=32,'narrow'=8] {'narrow'}, dimensions={0}, use_global_device_ids=true | all-gather | bytes 46080 | tf_op jit(solution)/shard_map/all_gather | solution.py:44
  182.6 66.8 %all-gather.7.cloned.1.call-done = bf16[160,4096]{1,0:T(8,128)(2,1)} async-done(((bf16[160,128]{1,0:T(8,128)(2,1)}), bf16[160,4096]{1,0:T(8,128)(2,1)}) %all-gather.7.cloned.1.call-update) | async-done | bytes 1310736 | tf_op jit(solution)/shard_map/all_gather | solution.py:48
  253.4 4.4 reshape.221
  270.6 6.2 fusion.4
  279.7 75.1 %pmax.7 = f32[160,32]{0,1:T(8,128)S(1)} all-reduce(f32[160,32]{0,1:T(8,128)S(1)} %copy.171), channel_id=1, replica_groups=mesh['wide'=32,'narrow'=8] {'wide','narrow'}, use_global_device_ids=true, to_apply=%region_5.7 | all-reduce | flops 5120 | bytes 40960 | tf_op jit(solution)/shard_map/pmax | solution.py:135
  357.6 5.5 broadcast_multiply_fusion
  363.1 5.1 copy.166
  368.2 6.7 reshape.223
  374.9 7.3 %dot_general.39 = f32[4,8,5,128,64]{3,2,1,0,4:T(8,128)} reshape(f32[20480,64]{0,1:T(8,128)} %bitcast.125) | data formatting | bytes 10485760 | tf_op jit(solution)/shard_map/dot_general | solution.py:103
  382.3 8.2 %fusion.17 = f32[32,5,4,8,128]{4,0,1,3,2:T(8,128)S(1)} fusion(f32[4,8,5,128,64]{3,2,1,0,4:T(8,128)} %dot_general.39, s32[64]{0:T(128)S(1)} %eq.48), kind=kOutput, calls=%fused_computation.30 | convolution fusion | flops 503318528 | bytes 7864576 | tf_op jit(solution)/shard_map/dot_general | solution.py:103
  402.7 12.8 %all-gather.3 = bf16[8,20,32]{2,1,0:T(8,128)(2,1)S(1)} all-gather(bf16[1,20,32]{2,1,0:T(8,128)(2,1)S(1)} %copy.173), channel_id=1, replica_groups=mesh['wide'=32,'narrow'=8] {'narrow'}, dimensions={0}, use_global_device_ids=true | all-gather | bytes 11520 | tf_op jit(solution)/shard_map/all_gather | solution.py:45
  415.6 47.0 %all_gather.25 = bf16[160,1024]{0,1:T(8,128)(2,1)S(1)} all-gather(bf16[160,32]{0,1:T(8,128)(2,1)S(1)} %copy.207), channel_id=1, replica_groups=mesh['wide'=32,'narrow'=8] {'wide'}, dimensions={1}, use_global_device_ids=true | all-gather | bytes 337920 | tf_op jit(solution)/shard_map/all_gather | solution.py:49
  465.8 6.4 fusion.20
  481.1 23.9 %all-reduce.1 = bf16[160,32]{1,0:T(8,128)(2,1)S(1)} all-reduce(bf16[160,32]{1,0:T(8,128)(2,1)S(1)} %copy.194), channel_id=5, replica_groups=mesh['wide'=32,'narrow'=8] {'narrow'}, use_global_device_ids=true, to_apply=%region_10.12.clone | all-reduce | flops 5120 | bytes 20480
  505.2 48.1 %all-gather.4 = bf16[32,160,4]{1,2,0:T(4,128)(2,1)S(1)} all-gather(bf16[1,160,4]{1,2,0:T(4,128)(2,1)S(1)} %copy.195), channel_id=2, replica_groups=mesh['wide'=32,'narrow'=8] {'wide'}, dimensions={0}, use_global_device_ids=true | all-gather | bytes 42240 | tf_op jit(solution)/shard_map/all_gather | solution.py:148
  555.4 136.7 %all-reduce.5.cloned.1.call-done = bf16[160,4,128]{2,1,0:T(4,128)(2,1)} async-done(((bf16[160,4,128]{2,1,0:T(4,128)(2,1)}), bf16[160,4,128]{2,1,0:T(4,128)(2,1)}) %all-reduce.5.cloned.1.call-update) | async-done | bytes 163856 | tf_op jit(solution)/shard_map/psum | solution.py:147
  694.1 23.9 %all-reduce.2 = bf16[160,128]{1,0:T(8,128)(2,1)S(1)} all-reduce(bf16[160,128]{1,0:T(8,128)(2,1)S(1)} %convolution_convert_fusion), channel_id=6, replica_groups=mesh['wide'=32,'narrow'=8] {'narrow'}, use_global_device_ids=true, to_apply=%region_13.15.clone | all-reduce | flops 20480 | bytes 81920
  (151 shorter events, 71.0 us)
Async XLA Ops:
  7.2 17.9 %copy-start = (bf16[64,16,1024]{2,1,0:T(8,128)(2,1)S(1)}, bf16[64,16,1024]{2,1,0:T(8,128)(2,1)}, u32[]{:S(2)}) copy-start(bf16[64,16,1024]{2,1,0:T(8,128)(2,1)} %param.16) | copy-start | bytes 6291460
  12.6 20.2 %all-to-all-start = ((s32[32,2,1]{1,2,0:T(1,128)}), s32[32,2,1]{1,2,0:T(1,128)S(1)}, u32[]{:S(2)}, u32[]{:S(2)}) async-start(s32[32,2,1]{1,2,0:T(1,128)} %bitcast.1), calls=%async_computation | async-start | bytes 32768 | tf_op jit(solution)/shard_map/all_to_all | solution.py:64
  32.7 13.6 %all-to-all-start.1 = ((s32[32,2,1]{1,2,0:T(1,128)}), s32[32,2,1]{1,2,0:T(1,128)S(1)}, u32[]{:S(2)}, u32[]{:S(2)}) async-start(s32[32,2,1]{1,2,0:T(1,128)} %bitcast.4), calls=%async_computation.1 | async-start | bytes 32768 | tf_op jit(solution)/shard_map/all_to_all | solution.py:67
  40.9 11.2 %copy-start.12 = (bf16[5,512]{1,0:T(8,128)(2,1)S(1)}, bf16[5,512]{1,0:T(8,128)(2,1)}, u32[]{:S(2)}) copy-start(bf16[5,512]{1,0:T(8,128)(2,1)} %param.12) | copy-start | bytes 15364
  40.9 97.6 %copy-start.10 = (bf16[512,32]{0,1:T(8,128)(2,1)S(1)}, bf16[512,32]{0,1:T(8,128)(2,1)}, u32[]{:S(2)}) copy-start(bf16[512,32]{0,1:T(8,128)(2,1)} %param.14) | copy-start | bytes 98308
  40.9 97.8 %copy-start.18 = (u32[256]{0:T(256)S(1)}, u32[256]{0:T(256)}, u32[]{:S(2)}) copy-start(u32[256]{0:T(256)} %constant.106) | copy-start | bytes 3076
  40.9 99.0 %copy-start.16 = (bf16[512,128]{1,0:T(8,128)(2,1)S(1)}, bf16[512,128]{1,0:T(8,128)(2,1)}, u32[]{:S(2)}) copy-start(bf16[512,128]{1,0:T(8,128)(2,1)} %param.13) | copy-start | bytes 393220
  40.9 140.8 %copy-start.2 = (s32[32]{0:T(128)S(1)}, s32[32]{0:T(128)}, u32[]{:S(2)}) copy-start(s32[32]{0:T(128)} %param.19) | copy-start | bytes 388
  46.3 207.1 %all-to-all-start.2 = ((bf16[64,16,1024]{2,1,0:T(8,128)(2,1)}), bf16[64,16,1024]{2,1,0:T(8,128)(2,1)}, u32[]{:S(2)}, u32[]{:S(2)}) async-start(bf16[64,16,1024]{2,1,0:T(8,128)(2,1)} %broadcast_select_fusion.1), calls=%async_computation.2 | async-start | bytes 4194304 | tf_op jit(solution)/shard_map/all_to_all | solution.py:61
  52.0 197.5 %all-gather.7.cloned.1.call-start = ((), (), s32[]{:S(2)}) async-start(), calls=%async_computation.4 | async-start | bytes 1351680 | tf_op jit(solution)/shard_map/all_gather | solution.py:48
  165.3 84.1 %copy-start.8 = (bf16[20,160]{0,1:T(8,128)(2,1)}, bf16[20,160]{0,1:T(8,128)(2,1)S(1)}, u32[]{:S(2)}) copy-start(bf16[20,160]{0,1:T(8,128)(2,1)S(1)} %dynamic-slice_convert_fusion) | copy-start | bytes 19204
  178.9 374.5 %reduce-scatter.4.cloned.1.call-start = ((), (), s32[]{:S(2)}) async-start(), calls=%async_computation.5 | async-start | bytes 1474560 | tf_op jit(solution)/shard_map/reduce_scatter | solution.py:139
  180.8 201.5 %copy-start.11 = (s32[64]{0:T(128)}, s32[64]{0:T(128)S(1)}, u32[]{:S(2)}) copy-start(s32[64]{0:T(128)S(1)} %eq.48) | copy-start | bytes 772
  181.7 71.8 %copy-start.15 = (s32[64]{0:T(128)}, s32[64]{0:T(128)S(1)}, u32[]{:S(2)}) copy-start(s32[64]{0:T(128)S(1)} %all_to_all.21) | copy-start | bytes 772
  182.5 96.2 %copy-start.13 = (pred[64]{0:T(512)(128)(4,1)}, pred[64]{0:T(512)(128)(4,1)S(1)}, u32[]{:S(2)}) copy-start(pred[64]{0:T(512)(128)(4,1)S(1)} %get-tuple-element.22) | copy-start | bytes 196
  257.9 3.7 copy-start.6
  270.6 8.0 %copy-start.7 = (f32[64,4,8,5]{0,3,2,1:T(8,128)S(1)}, f32[64,4,8,5]{0,3,2,1:T(8,128)}, u32[]{:S(2)}) copy-start(f32[64,4,8,5]{0,3,2,1:T(8,128)} %copy.189) | copy-start | bytes 122884
  276.8 2.6 copy-start.5
  278.7 76.2 %copy-start.14 = (pred[64]{0:T(512)(128)(4,1)S(1)}, pred[64]{0:T(512)(128)(4,1)}, u32[]{:S(2)}) copy-start(pred[64]{0:T(512)(128)(4,1)} %copy-done.13) | copy-start | bytes 196
  397.5 1.7 copy-start.3
  401.8 62.0 %copy-start.17 = (s32[32]{0:T(128)S(1)}, s32[32]{0:T(128)}, u32[]{:S(2)}) copy-start(s32[32]{0:T(128)} %param.21) | copy-start | bytes 388
  401.8 290.3 %all-reduce.5.cloned.1.call-start = ((), (), s32[]{:S(2)}) async-start(), calls=%async_computation.6 | async-start | bytes 327680 | tf_op jit(solution)/shard_map/psum | solution.py:147
  479.1 214.8 %copy-start.9 = (bf16[512,128]{1,0:T(8,128)(2,1)S(1)}, bf16[512,128]{1,0:T(8,128)(2,1)}, u32[]{:S(2)}) copy-start(bf16[512,128]{1,0:T(8,128)(2,1)} %param.15) | copy-start | bytes 393220
  692.1 29.8 %copy-start.1 = (bf16[64,16,1024]{2,1,0:T(8,128)(2,1)S(1)}, bf16[64,16,1024]{2,1,0:T(8,128)(2,1)}, u32[]{:S(2)}) copy-start(bf16[64,16,1024]{2,1,0:T(8,128)(2,1)} %param.16) | copy-start | bytes 6291460
  (1 other events, 0.8 us)
Sparse Core Ops, SparseCore 0:
  179.0 70.3 all-gather.6
  401.9 30.6 reduce-scatter.3
  555.1 136.8 all-reduce.4
